TPU v7x, 32 devices: a whole 2x2x4 slice. The times are simulated.
32 devices in a mesh: batch: 8 (over z, x), rep: 4 (over y, core).
Axes of the slice: x: 2, y: 2, z: 4, core: 2. Of those that a mesh axis runs over, the one named last changes fastest.
Arguments:
- latents: bfloat16 [4, 16, 512, 1024], P('rep', 'batch'), may hold values from -6 to 6
- query_key_value_weight: bfloat16 [1024, 3072], P('batch'), may hold values from -0.1875 to 0.1875
- output_weight: bfloat16 [1024, 1024], P('batch'), may hold values from -1.5 to 1.5
- up_weight: bfloat16 [1024, 1024], P('batch'), may hold values from -0.1875 to 0.1875
- down_weight: bfloat16 [1024, 1024], P('batch'), may hold values from -0.1875 to 0.1875
- norm_gains: bfloat16 [2, 1024], P(None, 'batch'), may hold values from 0.099609375 to 1.8984375
- biases: bfloat16 [6, 1024], P(None, 'batch'), may hold values from -1.5 to 1.5
- feed_forward_bias: bfloat16 [1024], P('batch'), may hold values from -1.5 to 1.5
- cotangent: bfloat16 [4, 16, 512, 1024], P('rep', 'batch'), may hold values from -6 to 6
Outputs:
- out_latents: bfloat16 [4, 16, 512, 1024], P('rep', 'batch')
- grad_latents: bfloat16 [4, 16, 512, 1024], P('rep', 'batch')
- grad_w_qkv: float32 [1024, 3072], P('batch')
- grad_w_out: float32 [1024, 1024], P('batch')
- grad_w_up: float32 [1024, 1024], P('batch')
- grad_w_down: float32 [1024, 1024], P('batch')
- grad_gains: float32 [2, 1024], P(None, 'batch')
- grad_biases: float32 [6, 1024], P(None, 'batch')
- grad_mlp_bias: float32 [1024], P('batch')
All inputs are finite; a program needn't handle non-finite values.
Results may differ from a plain program's by a relative error of at most 0.014.
The roundings to bfloat16 on the way count: a program that leaves them out, or rounds other values in their place, can miss the bound.
Values may be sent and summed in bfloat16 or wider, within the bound.
No kernel may reach another device: no remote copies, remote signals or barrier semaphores. Data moves between devices by JAX's collectives and lax.ppermute only.
A program may use at most 192 MiB of HBM per device.

v0:
```python
import jax
import jax.numpy as jnp
from jax import lax
from jax.sharding import PartitionSpec as P

HEADS = 8
EPS = 1e-05
AXES = ("batch", "rep")
BF = jnp.bfloat16
F32 = jnp.float32


def layer_norm(values, gain, shift):
    mean = jnp.mean(values, axis=-1, keepdims=True)
    centred = values - mean
    spread = jnp.mean(centred * centred, axis=-1, keepdims=True)
    return centred * lax.rsqrt(spread + EPS) * gain + shift


def permutation(move, nb, nr):
    pairs = []
    for b in range(nb):
        for r in range(nr):
            tb, tr = move(b, r)
            pairs.append((b * nr + r, tb * nr + tr))
    return pairs


class Links:

    def __init__(self, nb, nr):

        def swap(kb, kr):
            return permutation(lambda b, r: (b ^ kb, r ^ kr), nb, nr)

        self.core = swap(0, 1)
        self.rep = [swap(0, 1), swap(0, 2), swap(0, 3)]
        self.z = [swap(2, 0), swap(4, 0), swap(6, 0)]
        self.y_or_x = permutation(lambda b, r: (b, r ^ 2) if r % 2 == 0 else (b ^ 1, r), nb, nr)
        self.x_or_y = permutation(lambda b, r: (b ^ 1, r) if r % 2 == 0 else (b, r ^ 2), nb, nr)
        batch, rep = (lax.axis_index("batch"), lax.axis_index("rep"))
        self.xi, self.zi = (batch % 2, batch // 2)
        self.ci, self.yi = (rep % 2, rep // 2)


def move(value, pairs):
    return lax.ppermute(value, AXES, pairs)


def flip_if(bit, value, axis):
    return jnp.where(bit == 1, jnp.flip(value, axis), value)


def gather_rows(local, links):
    rows, n = local.shape
    quarter = lax.dynamic_index_in_dim(
        local.reshape(4, rows // 4, n), links.ci * 2 + links.yi, 0, keepdims=False
    )
    own = jnp.stack([quarter] + [move(quarter, p) for p in links.z])
    first = move(own, links.y_or_x)
    second = move(own, links.x_or_y)
    third = move(first, links.x_or_y)
    halves = []
    here = [own, first, second, third]
    there = [move(part, links.core) for part in here]
    for parts, core in ((here, links.ci), (there, 1 - links.ci)):
        a, f, s, t = parts
        dx = jnp.where(core == 1, f, s)
        dy = jnp.where(core == 1, s, f)
        halves.append(jnp.stack([jnp.stack([a, dy]), jnp.stack([dx, t])]))
    whole = jnp.stack(halves)
    whole = flip_if(links.ci, whole, 0)
    whole = flip_if(links.xi, whole, 1)
    whole = flip_if(links.yi, whole, 2)
    whole = flip_if(links.zi % 2, whole.reshape(2, 2, 2, 2, 2, rows // 4, n), 4)
    whole = flip_if(links.zi // 2, whole, 3)
    whole = whole.transpose(3, 4, 1, 0, 2, 5, 6)
    return whole.reshape(8 * rows, n)


def reduce_rows(partial, links):
    total, n = partial.shape
    rows, q = (total // 8, n // 4)
    view = partial.reshape(4, 2, rows, 2, 2, q)
    view = view.transpose(3, 1, 4, 0, 2, 5)
    keep = lax.dynamic_index_in_dim(view, links.ci, 0, keepdims=False)
    send = lax.dynamic_index_in_dim(view, 1 - links.ci, 0, keepdims=False).astype(BF)
    held = keep + move(send, links.core).astype(F32)
    held = jnp.where(links.ci == 0, held, held.transpose(1, 0, 2, 3, 4))
    mine = jnp.where(links.ci == 0, links.xi, links.yi)
    keep = lax.dynamic_index_in_dim(held, mine, 0, keepdims=False)
    send = lax.dynamic_index_in_dim(held, 1 - mine, 0, keepdims=False).astype(BF)
    held = keep + move(send, links.x_or_y).astype(F32)
    mine = jnp.where(links.ci == 0, links.yi, links.xi)
    keep = lax.dynamic_index_in_dim(held, mine, 0, keepdims=False)
    send = lax.dynamic_index_in_dim(held, 1 - mine, 0, keepdims=False).astype(BF)
    held = keep + move(send, links.y_or_x).astype(F32)
    out = lax.dynamic_index_in_dim(held, links.zi, 0, keepdims=False)
    for k, pairs in enumerate(links.z):
        send = lax.dynamic_index_in_dim(held, links.zi ^ k + 1, 0, keepdims=False).astype(BF)
        out = out + move(send, pairs).astype(F32)
    out = out.astype(BF)
    by_core, by_y, by_both = [move(out, p) for p in links.rep]
    grid = jnp.stack([jnp.stack([out, by_y]), jnp.stack([by_core, by_both])])
    grid = flip_if(links.yi, flip_if(links.ci, grid, 0), 1)
    return grid.transpose(2, 0, 1, 3).reshape(rows, n).astype(F32)


def heads_of(packed):
    images, length, width = packed.shape
    size = width // 3 // HEADS
    view = packed.reshape(images, length, 3, HEADS, size)
    return (view[:, :, 0], view[:, :, 1], view[:, :, 2], size ** (-0.5))


def per_device(latents, w_qkv, w_out, w_up, w_down, gains, biases, ff_bias, cotangent, *, nb, nr):
    reps, images, length, width = latents.shape
    x = latents.reshape(-1, width).astype(F32)
    cot = cotangent.reshape(-1, width)
    count = reps * images
    small = jnp.concatenate([gains, biases, ff_bias[None]], axis=0)
    native = nb != 8 or nr != 4
    if native:
        small = lax.all_gather(small, "batch", axis=1, tiled=True)
        w_qkv, w_out, w_up, w_down = (
            lax.all_gather(w, "batch", axis=0, tiled=True) for w in (w_qkv, w_out, w_up, w_down)
        )
    else:
        links = Links(nb, nr)
        small = lax.all_gather(small, "batch", axis=1, tiled=True)
        w_qkv = gather_rows(w_qkv, links)
        rest = gather_rows(jnp.concatenate([w_out, w_up, w_down], axis=1), links)
        w_out, w_up, w_down = (rest[:, :width], rest[:, width:-width], rest[:, -width:])
    small = small.astype(F32)
    g1, g2 = (small[0], small[1])
    b1, bq, bv, bo, b2, bd, bu = (small[i] for i in range(2, 9))

    def dot(a, b, dims):
        return lax.dot_general(a, b, (dims, ((), ())), preferred_element_type=F32)

    NN, NT, TN = (((1,), (0,)), ((1,), (1,)), ((0,), (0,)))
    first, pull_one = jax.vjp(layer_norm, x, g1, b1)
    first = first.astype(BF)
    packed = dot(first, w_qkv, NN) + jnp.concatenate([bq, jnp.zeros_like(bq), bv])
    packed = packed.astype(BF).reshape(count, length, 3 * width)
    q, k, v, scale = heads_of(packed)
    scores = jnp.einsum("iqhd,ikhd->ihqk", q, k, preferred_element_type=F32) * scale
    top = jnp.max(scores, axis=-1, keepdims=True)
    raised = jnp.exp(scores - top)
    p = raised / jnp.sum(raised, axis=-1, keepdims=True)
    probs = p.astype(BF)
    mixed = jnp.einsum("ihqk,ikhd->iqhd", probs, v, preferred_element_type=F32)
    mixed = mixed.astype(BF).reshape(-1, width)
    middle = x + dot(mixed, w_out, NN) + bo
    second, pull_two = jax.vjp(layer_norm, middle, g2, b2)
    second = second.astype(BF)
    hidden = dot(second, w_up, NN) + bu
    active, pull_gelu = jax.vjp(jax.nn.gelu, hidden)
    active = active.astype(BF)
    out = (middle + dot(active, w_down, NN) + bd).astype(BF)
    gw_down = dot(active, cot, TN)
    gb_down = jnp.sum(cot.astype(F32), axis=0)
    g_hidden = pull_gelu(dot(cot, w_down, NT))[0].astype(BF)
    gw_up = dot(second, g_hidden, TN)
    gb_up = jnp.sum(g_hidden.astype(F32), axis=0)
    g_mid, gg2, gb2 = pull_two(dot(g_hidden, w_up, NT))
    g_middle = cot.astype(F32) + g_mid
    g_attn = g_middle.astype(BF)
    gw_out = dot(mixed, g_attn, TN)
    gb_out = jnp.sum(g_attn.astype(F32), axis=0)
    g_mixed = dot(g_attn, w_out, NT).astype(BF).reshape(count, length, HEADS, -1)
    g_v = jnp.einsum("ihqk,iqhd->ikhd", probs, g_mixed, preferred_element_type=F32)
    g_p = jnp.einsum("iqhd,ikhd->ihqk", g_mixed, v, preferred_element_type=F32)
    g_s = (p * (g_p - jnp.sum(g_p * p, axis=-1, keepdims=True))).astype(BF)
    g_q = jnp.einsum("ihqk,ikhd->iqhd", g_s, k, preferred_element_type=F32) * scale
    g_k = jnp.einsum("ihqk,iqhd->ikhd", g_s, q, preferred_element_type=F32) * scale
    g_packed = jnp.stack([g_q, g_k, g_v], axis=2).astype(BF).reshape(-1, 3 * width)
    gw_qkv = dot(first, g_packed, TN)
    gb_packed = jnp.sum(g_packed.astype(F32), axis=0)
    g_in, gg1, gb1 = pull_one(dot(g_packed, w_qkv, NT))
    g_lat = (g_middle + g_in).astype(BF)
    zero = jnp.zeros_like(gb_up)
    smalls = jnp.stack(
        [gg1, gg2, gb1, gb_packed[:width], gb_packed[2 * width :], gb_out, gb2, gb_down, gb_up]
        + [zero] * 7
    )
    smalls = lax.psum(smalls, AXES)
    smalls = lax.dynamic_slice_in_dim(
        smalls, lax.axis_index("batch") * (width // nb), width // nb, 1
    )
    if native:

        def reduced(g):
            g = lax.psum_scatter(g, "batch", scatter_dimension=0, tiled=True)
            return lax.psum(g.astype(BF), "rep").astype(F32)

        gw_qkv, gw_out, gw_up, gw_down = (reduced(g) for g in (gw_qkv, gw_out, gw_up, gw_down))
    else:
        rest = reduce_rows(jnp.concatenate([gw_out, gw_up, gw_down], axis=1), links)
        gw_qkv = reduce_rows(gw_qkv, links)
        gw_out, gw_up, gw_down = (rest[:, :width], rest[:, width:-width], rest[:, -width:])
    return (
        out.reshape(latents.shape),
        g_lat.reshape(latents.shape),
        gw_qkv,
        gw_out,
        gw_up,
        gw_down,
        smalls[:2],
        smalls[2:8],
        smalls[8],
    )


def solution(mesh):
    nb, nr = (mesh.shape["batch"], mesh.shape["rep"])

    def body(*args):
        return per_device(*args, nb=nb, nr=nr)

    rows = P("batch", None)
    cols = P(None, "batch")
    data = P("rep", "batch", None, None)
    return jax.shard_map(
        body,
        mesh=mesh,
        in_specs=(data, rows, rows, rows, rows, cols, cols, P("batch"), data),
        out_specs=(data, data, rows, rows, rows, rows, cols, cols, P("batch")),
        check_vma=False,
    )
```

profile of v0, /device:TPU:0, one launch (start us, length us, event | category | flops | bytes accessed | tf_op | source)
XLA Modules:
  0.0 650.0 jit_solution(16085910962180508302)
XLA Ops:
  20.9 45.8 %all_gather.3 = bf16[9,1024]{1,0:T(8,128)(2,1)S(1)} all-gather(bf16[9,128]{1,0:T(8,128)(2,1)S(1)} %pad_maximum_fusion.9), channel_id=1, replica_groups=mesh['batch'=8,'rep'=4] {'batch'}, dimensions={1}, use_global_device_ids=true | all-gather | bytes 20736 | tf_op jit(solution)/shard_map/all_gather | solution.py:130
  89.4 12.0 %collective-permute-done.14 = bf16[4,32,3072]{2,1,0:T(8,128)(2,1)S(1)} collective-permute-done((bf16[4,32,3072]{2,1,0:T(8,128)(2,1)S(1)}, bf16[4,32,3072]{2,1,0:T(8,128)(2,1)S(1)}, u32[]{:S(2)}, u32[]{:S(2)}) %collective-permute-start.14) | collective-permute-done | bytes 786464 | tf_op jit(solution)/shard_map/ppermute | solution.py:47
  107.8 8.4 %collective-permute-done.15 = bf16[4,32,3072]{2,1,0:T(8,128)(2,1)} collective-permute-done((bf16[4,32,3072]{2,1,0:T(8,128)(2,1)S(1)}, bf16[4,32,3072]{2,1,0:T(8,128)(2,1)}, u32[]{:S(2)}, u32[]{:S(2)}) %collective-permute-start.15) | collective-permute-done | bytes 786464 | tf_op jit(solution)/shard_map/ppermute | solution.py:47
  147.0 7.6 %reverse_select_fusion.7 = bf16[2,2,2,4,32,3072]{5,4,2,0,1,3:T(8,128)(2,1)S(1)} fusion(bf16[2,2,2,4,32,3072]{5,4,2,0,1,3:T(8,128)(2,1)} %reverse_select_fusion.8, pred[]{:T(512)S(6)} %eq.21), kind=kLoop, calls=%fused_computation.17 | loop fusion | flops 3145728 | bytes 12582913 | tf_op jit(solution)/shard_map/jit(_where)/select_n | solution.py:51
  181.3 8.6 %fusion.5 = bf16[128,8,24,128]{3,1,2,0:T(8,128)(2,1)} fusion(f32[3072]{0:T(1024)S(1)} %pad_maximum_fusion.8, bf16[1024,1024]{1,0:T(8,128)(2,1)S(1)} %bitcast.349, bf16[1024,3072]{1,0:T(8,128)(2,1)S(1)} %bitcast.343), kind=kOutput, calls=%fused_computation.22 | convolution fusion | flops 6448742400 | bytes 14692352 | tf_op jit(solution)/shard_map/dot_general | solution.py:139
  202.3 10.4 %fusion.52 = f32[2,8,512,512]{2,3,1,0:T(8,128)} fusion(bf16[2,512,1,8,128]{4,3,2,1,0:T(8,128)(2,1)} %get-tuple-element.33, bf16[2,512,1,8,128]{4,3,2,1,0:T(8,128)(2,1)} %get-tuple-element.31), kind=kOutput, calls=%fused_computation.106 | convolution fusion | flops 1073741824 | bytes 20971520 | tf_op jit(solution)/shard_map/iqhd,ikhd->ihqk/dot_general | solution.py:147
  212.6 18.9 %fusion.100 = (f32[2,8,512]{2,1,0:T(8,128)S(1)}, f32[2,8,512,512]{2,3,1,0:T(8,128)}) fusion(f32[2,8,512,512]{2,3,1,0:T(8,128)} %fusion.52), kind=kOutput, calls=%fused_computation.208 | output fusion | flops 16777728 | bytes 33587200 | tf_op jit(solution)/shard_map/sub | solution.py:149
  231.6 8.4 %convert_bitcast_fusion.2 = bf16[2,512,8,128]{1,3,2,0:T(8,128)(2,1)} fusion(bf16[2,512,1,8,128]{1,4,3,0,2:T(8,128)(2,1)S(1)} %copy-done.22, f32[2,8,512,512]{2,3,1,0:T(8,128)} %get-tuple-element.74, f32[2,8,512]{2,1,0:T(8,128)S(1)} %get-tuple-element.73), kind=kOutput, calls=%fused_computation.105 | convolution fusion | flops 1083179008 | bytes 21004288 | tf_op jit(solution)/shard_map/ihqk,ikhd->iqhd/dot_general | solution.py:152
  287.8 10.7 %fusion.38 = bf16[2,512,1,8,128]{1,4,3,0,2:T(8,128)(2,1)} fusion(bf16[2,512,8,128]{1,3,2,0:T(8,128)(2,1)} %copy.53, f32[2,8,512,512]{2,3,1,0:T(8,128)} %get-tuple-element.74, f32[2,8,512]{2,1,0:T(8,128)S(1)} %get-tuple-element.73), kind=kOutput, calls=%fused_computation.94 | convolution fusion | flops 1082130432 | bytes 21004288 | tf_op jit(solution)/shard_map/ihqk,iqhd->ikhd/dot_general | solution.py:172
  298.5 10.9 %multiply_reduce_fusion = (f32[2,8,512]{2,1,0:T(8,128)S(1)}, f32[2,8,512,512]{2,3,1,0:T(8,128)}) fusion(f32[2,8,512,512]{2,3,1,0:T(8,128)} %get-tuple-element.74, f32[2,8,512]{2,1,0:T(8,128)S(1)} %get-tuple-element.73, bf16[2,512,8,128]{1,3,2,0:T(8,128)(2,1)S(1)} %copy-done.25, bf16[2,512,1,8,128]{1,4,3,0,2:T(8,128)(2,1)S(1)} %copy-done.23), kind=kOutput, calls=%fused_computation.2 | convolution fusion | flops 1086316544 | bytes 37814272 | tf_op jit(solution)/shard_map/iqhd,ikhd->ihqk/dot_general | solution.py:173
  309.4 11.9 %multiply_convert_fusion = bf16[2,8,512,512]{2,3,1,0:T(8,128)(2,1)S(1)} fusion(f32[2,8,512,512]{2,3,1,0:T(8,128)} %get-tuple-element.79, f32[2,8,512]{2,1,0:T(8,128)S(1)} %get-tuple-element.78, f32[2,8,512,512]{2,3,1,0:T(8,128)} %get-tuple-element.74, f32[2,8,512]{2,1,0:T(8,128)S(1)} %get-tuple-element.73), kind=kLoop, calls=%fused_computation.1 | loop fusion | flops 16777216 | bytes 42008576 | tf_op jit(solution)/shard_map/convert_element_type | solution.py:174
  336.7 16.9 %reshape.232 = f32[4,2,128,2,2,768]{2,1,0,5,4,3:T(2,128)} reshape(f32[1024,3072]{0,1:T(8,128)} %pad_maximum_fusion) | data formatting | bytes 25165824 | tf_op jit(solution)/shard_map/reshape | solution.py:84
  360.1 8.7 %copy.89 = bf16[4,2,128,1,2,768]{5,2,0,1,4,3:T(8,128)(2,1)} copy(bf16[4,2,128,1,2,768]{2,1,0,5,4,3:T(2,128)(2,1)} %constant_dynamic-slice_fusion.1) | data formatting | bytes 6291456
  375.3 9.2 %copy.55 = bf16[2,512,3,8,128]{4,3,2,1,0:T(8,128)(2,1)} copy(bf16[2,512,3,8,128]{1,4,3,0,2:T(8,128)(2,1)} %get-tuple-element.28) | data formatting | bytes 12582912 | tf_op jit(solution)/shard_map/convert_element_type | solution.py:177
  384.5 10.3 %convert_element_type.247 = bf16[1024,3072]{1,0:T(8,128)(2,1)} reshape(bf16[2,512,3,8,128]{4,3,2,1,0:T(8,128)(2,1)} %copy.55) | data formatting | bytes 12582912 | tf_op jit(solution)/shard_map/convert_element_type | solution.py:177
  394.8 12.4 %fusion.93 = (f32[1024]{0:T(1024)S(1)}, f32[1024]{0:T(1024)S(1)}, f32[1024,1024]{1,0:T(8,128)}) fusion(f32[1024]{0:T(1024)S(1)} %bitcast.371, f32[1024]{0:T(1024)S(1)} %bitcast.376, bf16[1,2,512,1024]{3,2,1,0:T(8,128)(2,1)S(1)} %copy-done.2, bf16[1024,3072]{1,0:T(8,128)(2,1)} %convert_element_type.247, bf16[1024,3072]{1,0:T(8,128)(2,1)} %bitcast.344), kind=kOutput, calls=%fused_computation.202 | convolution fusion | flops 6448740352 | bytes 18890752 | tf_op jit(solution)/shard_map/dot_general | solution.py:139
  407.2 8.9 %copy.56 = bf16[3072,1024]{1,0:T(8,128)(2,1)} copy(bf16[3072,1024]{0,1:T(8,128)(2,1)} %bitcast.325) | data formatting | bytes 12582912 | tf_op jit(solution)/shard_map/dot_general | solution.py:139
  425.2 9.5 %fusion.102 = f32[4,2,128,2,2,768]{5,2,4,3,1,0:T(8,128)S(1)} fusion(bf16[4,2,128,1024,1,1]{3,2,5,4,1,0:T(8,128)(2,1)} %bitcast.352, bf16[2,2,768,1024,1,1]{3,2,1,0,5,4:T(8,128)(2,1)} %bitcast.345), kind=kOutput, calls=%fused_computation.210 | convolution fusion | flops 6442450944 | bytes 20971520 | tf_op jit(solution)/shard_map/dot_general | solution.py:139
  443.4 7.6 %constant_dynamic-slice_fusion.2 = f32[4,2,128,1,2,768]{2,1,0,5,4,3:T(2,128)} fusion(f32[4,2,128,2,2,768]{2,1,0,5,4,3:T(2,128)} %reshape.232, s32[]{:T(128)S(6)} %select_n.249), kind=kLoop, calls=%fused_computation.179 | loop fusion | bytes 12582916 | tf_op jit(solution)/shard_map/dynamic-slice.2
  451.0 10.5 %copy.88 = f32[4,2,128,1,2,768]{5,2,0,1,4,3:T(8,128)} copy(f32[4,2,128,1,2,768]{2,1,0,5,4,3:T(2,128)} %constant_dynamic-slice_fusion.2) | data formatting | bytes 12582912
  480.5 8.5 %add_convert_fusion.2 = bf16[1024,1024]{1,0:T(8,128)(2,1)} fusion(f32[1024,1024]{1,0:T(8,128)} %copy-done.10, f32[1024]{0:T(1024)S(1)} %bitcast.394, bf16[1024,3072]{1,0:T(8,128)(2,1)} %bitcast.336, f32[1024,1024]{1,0:T(8,128)} %copy-done.42, f32[1024]{0:T(1024)S(1)} %bitcast.393), kind=kOutput, calls=%fused_computation.75 | convolution fusion | flops 2161115136 | bytes 12591104 | tf_op jit(solution)/shard_map/dot_general | solution.py:139
  491.5 22.9 %collective-permute-done.21 = bf16[2,4,128,768]{3,2,0,1:T(8,128)(2,1)S(1)} collective-permute-done((bf16[2,4,128,768]{3,2,0,1:T(8,128)(2,1)S(1)}, bf16[2,4,128,768]{3,2,0,1:T(8,128)(2,1)S(1)}, u32[]{:S(2)}, u32[]{:S(2)}) %collective-permute-start.21) | collective-permute-done | bytes 1572896 | tf_op jit(solution)/shard_map/ppermute | solution.py:47
  520.9 58.8 %all-reduce.2.cloned.1.call-done = f32[16,1024]{1,0:T(8,128)} async-done(((f32[16,1024]{1,0:T(8,128)}), f32[16,1024]{1,0:T(8,128)}) %all-reduce.2.cloned.1.call-update) | async-done | bytes 65552 | tf_op jit(solution)/shard_map/psum | solution.py:187
  600.3 16.3 %collective-permute-done.33 = bf16[128,768]{1,0:T(8,128)(2,1)S(1)} collective-permute-done((bf16[128,768]{1,0:T(8,128)(2,1)S(1)}, bf16[128,768]{1,0:T(8,128)(2,1)S(1)}, u32[]{:S(2)}, u32[]{:S(2)}) %collective-permute-start.33) | collective-permute-done | bytes 196640 | tf_op jit(solution)/shard_map/ppermute | solution.py:47
  (287 shorter events, 280.5 us)
Async XLA Ops:
  7.2 572.5 %all-reduce.2.cloned.1.call-start = ((), (), s32[]{:S(2)}) async-start(), calls=%async_computation | async-start | bytes 131072 | tf_op jit(solution)/shard_map/psum | solution.py:187
  8.3 59.0 %collective-permute-start.2 = (bf16[32,3072]{1,0:T(8,128)(2,1)S(1)}, bf16[32,3072]{1,0:T(8,128)(2,1)S(1)}, u32[]{:S(2)}, u32[]{:S(2)}) collective-permute-start(bf16[32,3072]{1,0:T(8,128)(2,1)S(1)} %fusion.119), channel_id=1, source_target_pairs={{0,24},{1,25},{2,26},{3,27},{4,28},{5,29},{6,30},{7,31},{8,16},{9,... | collective-permute-start | bytes 589832 | tf_op jit(solution)/shard_map/ppermute | solution.py:47
  13.4 54.2 %collective-permute-start.1 = (bf16[32,3072]{1,0:T(8,128)(2,1)S(1)}, bf16[32,3072]{1,0:T(8,128)(2,1)S(1)}, u32[]{:S(2)}, u32[]{:S(2)}) collective-permute-start(bf16[32,3072]{1,0:T(8,128)(2,1)S(1)} %fusion.119), channel_id=1, source_target_pairs={{0,16},{1,17},{2,18},{3,19},{4,20},{5,21},{6,22},{7,23},{8,24},{9,... | collective-permute-start | bytes 589832 | tf_op jit(solution)/shard_map/ppermute | solution.py:47
  13.5 54.2 %collective-permute-start = (bf16[32,3072]{1,0:T(8,128)(2,1)S(1)}, bf16[32,3072]{1,0:T(8,128)(2,1)S(1)}, u32[]{:S(2)}, u32[]{:S(2)}) collective-permute-start(bf16[32,3072]{1,0:T(8,128)(2,1)S(1)} %fusion.119), channel_id=1, source_target_pairs={{0,8},{1,9},{2,10},{3,11},{4,12},{5,13},{6,14},{7,15},{8,0},{9,1},... | collective-permute-start | bytes 589832 | tf_op jit(solution)/shard_map/ppermute | solution.py:47
  16.0 57.5 %collective-permute-start.12 = (bf16[32,3072]{1,0:T(8,128)(2,1)}, bf16[32,3072]{1,0:T(8,128)(2,1)S(1)}, u32[]{:S(2)}, u32[]{:S(2)}) collective-permute-start(bf16[32,3072]{1,0:T(8,128)(2,1)} %fusion.120), channel_id=1, source_target_pairs={{0,24},{1,25},{2,26},{3,27},{4,28},{5,29},{6,30},{7,31},{8,16},{9,... | collective-permute-start | bytes 589832 | tf_op jit(solution)/shard_map/ppermute | solution.py:47
  19.7 53.9 %collective-permute-start.11 = (bf16[32,3072]{1,0:T(8,128)(2,1)}, bf16[32,3072]{1,0:T(8,128)(2,1)S(1)}, u32[]{:S(2)}, u32[]{:S(2)}) collective-permute-start(bf16[32,3072]{1,0:T(8,128)(2,1)} %fusion.120), channel_id=1, source_target_pairs={{0,16},{1,17},{2,18},{3,19},{4,20},{5,21},{6,22},{7,23},{8,24},{9,... | collective-permute-start | bytes 589832 | tf_op jit(solution)/shard_map/ppermute | solution.py:47
  68.6 16.0 %collective-permute-start.4 = (bf16[4,32,3072]{2,1,0:T(8,128)(2,1)}, bf16[4,32,3072]{2,1,0:T(8,128)(2,1)}, u32[]{:S(2)}, u32[]{:S(2)}) collective-permute-start(bf16[4,32,3072]{2,1,0:T(8,128)(2,1)} %get-tuple-element.53), channel_id=1, source_target_pairs={{0,2},{1,5},{2,0},{3,7},{4,6},{5,1},{6,4},{7,3},{8,10},{9,13},{10,... | collective-permute-start | bytes 2359304 | tf_op jit(solution)/shard_map/ppermute | solution.py:47
  70.1 17.6 %collective-permute-start.3 = (bf16[4,32,3072]{2,1,0:T(8,128)(2,1)}, bf16[4,32,3072]{2,1,0:T(8,128)(2,1)}, u32[]{:S(2)}, u32[]{:S(2)}) collective-permute-start(bf16[4,32,3072]{2,1,0:T(8,128)(2,1)} %get-tuple-element.53), channel_id=1, source_target_pairs={{0,4},{1,3},{2,6},{3,1},{4,0},{5,7},{6,2},{7,5},{8,12},{9,11},{10,... | collective-permute-start | bytes 2359304 | tf_op jit(solution)/shard_map/ppermute | solution.py:47
  73.5 48.8 %collective-permute-start.6 = (bf16[4,32,3072]{2,1,0:T(8,128)(2,1)}, bf16[4,32,3072]{2,1,0:T(8,128)(2,1)S(1)}, u32[]{:S(2)}, u32[]{:S(2)}) collective-permute-start(bf16[4,32,3072]{2,1,0:T(8,128)(2,1)} %get-tuple-element.53), channel_id=1, source_target_pairs={{0,1},{1,0},{2,3},{3,2},{4,5},{5,4},{6,7},{7,6},{8,9},{9,8},{10,11... | collective-permute-start | bytes 2359304 | tf_op jit(solution)/shard_map/ppermute | solution.py:47
  74.7 26.7 %collective-permute-start.14 = (bf16[4,32,3072]{2,1,0:T(8,128)(2,1)S(1)}, bf16[4,32,3072]{2,1,0:T(8,128)(2,1)S(1)}, u32[]{:S(2)}, u32[]{:S(2)}) collective-permute-start(bf16[4,32,3072]{2,1,0:T(8,128)(2,1)S(1)} %get-tuple-element.55), channel_id=1, source_target_pairs={{0,2},{1,5},{2,0},{3,7},{4,6},{5,1},{6,4},{7,3},{8,10},{9,13},{10,... | collective-permute-start | bytes 2359304 | tf_op jit(solution)/shard_map/ppermute | solution.py:47
  76.0 25.4 %collective-permute-start.13 = (bf16[4,32,3072]{2,1,0:T(8,128)(2,1)S(1)}, bf16[4,32,3072]{2,1,0:T(8,128)(2,1)S(1)}, u32[]{:S(2)}, u32[]{:S(2)}) collective-permute-start(bf16[4,32,3072]{2,1,0:T(8,128)(2,1)S(1)} %get-tuple-element.55), channel_id=1, source_target_pairs={{0,4},{1,3},{2,6},{3,1},{4,0},{5,7},{6,2},{7,5},{8,12},{9,11},{10,... | collective-permute-start | bytes 2359304 | tf_op jit(solution)/shard_map/ppermute | solution.py:47
  84.6 23.0 %collective-permute-start.5 = (bf16[4,32,3072]{2,1,0:T(8,128)(2,1)}, bf16[4,32,3072]{2,1,0:T(8,128)(2,1)S(1)}, u32[]{:S(2)}, u32[]{:S(2)}) collective-permute-start(bf16[4,32,3072]{2,1,0:T(8,128)(2,1)} %collective-permute-done.4), channel_id=1, source_target_pairs={{0,4},{1,3},{2,6},{3,1},{4,0},{5,7},{6,2},{7,5},{8,12},{9,11},{10,... | collective-permute-start | bytes 2359304 | tf_op jit(solution)/shard_map/ppermute | solution.py:47
  87.7 29.7 %collective-permute-start.8 = (bf16[4,32,3072]{2,1,0:T(8,128)(2,1)}, bf16[4,32,3072]{2,1,0:T(8,128)(2,1)S(1)}, u32[]{:S(2)}, u32[]{:S(2)}) collective-permute-start(bf16[4,32,3072]{2,1,0:T(8,128)(2,1)} %collective-permute-done.4), channel_id=1, source_target_pairs={{0,1},{1,0},{2,3},{3,2},{4,5},{5,4},{6,7},{7,6},{8,9},{9,8},{10,11... | collective-permute-start | bytes 2359304 | tf_op jit(solution)/shard_map/ppermute | solution.py:47
  101.4 16.6 %collective-permute-start.7 = (bf16[4,32,3072]{2,1,0:T(8,128)(2,1)}, bf16[4,32,3072]{2,1,0:T(8,128)(2,1)S(1)}, u32[]{:S(2)}, u32[]{:S(2)}) collective-permute-start(bf16[4,32,3072]{2,1,0:T(8,128)(2,1)} %collective-permute-done.3), channel_id=1, source_target_pairs={{0,1},{1,0},{2,3},{3,2},{4,5},{5,4},{6,7},{7,6},{8,9},{9,8},{10,11... | collective-permute-start | bytes 2359304 | tf_op jit(solution)/shard_map/ppermute | solution.py:47
  368.8 94.1 %collective-permute-start.29 = (bf16[2,2,4,128,768]{4,3,2,0,1:T(8,128)(2,1)}, bf16[2,2,4,128,768]{4,3,2,0,1:T(8,128)(2,1)}, u32[]{:S(2)}, u32[]{:S(2)}) collective-permute-start(bf16[2,2,4,128,768]{4,3,2,0,1:T(8,128)(2,1)} %bitcast.348), channel_id=1, source_target_pairs={{0,1},{1,0},{2,3},{3,2},{4,5},{5,4},{6,7},{7,6},{8,9},{9,8},{10,11... | collective-permute-start | bytes 9437192 | tf_op jit(solution)/shard_map/ppermute | solution.py:47
  441.3 28.1 %collective-permute-start.20 = (bf16[2,2,4,128,768]{4,3,1,0,2:T(8,128)(2,1)}, bf16[2,2,4,128,768]{4,3,1,0,2:T(8,128)(2,1)}, u32[]{:S(2)}, u32[]{:S(2)}) collective-permute-start(bf16[2,2,4,128,768]{4,3,1,0,2:T(8,128)(2,1)} %fusion.36), channel_id=1, source_target_pairs={{0,1},{1,0},{2,3},{3,2},{4,5},{5,4},{6,7},{7,6},{8,9},{9,8},{10,11... | collective-permute-start | bytes 9437192 | tf_op jit(solution)/shard_map/ppermute | solution.py:47
  468.2 20.8 %collective-permute-start.30 = (bf16[2,4,128,768]{3,2,1,0:T(8,128)(2,1)S(1)}, bf16[2,4,128,768]{3,2,1,0:T(8,128)(2,1)S(1)}, u32[]{:S(2)}, u32[]{:S(2)}) collective-permute-start(bf16[2,4,128,768]{3,2,1,0:T(8,128)(2,1)S(1)} %fusion.68), channel_id=1, source_target_pairs={{0,4},{1,3},{2,6},{3,1},{4,0},{5,7},{6,2},{7,5},{8,12},{9,11},{10,... | collective-permute-start | bytes 4718600 | tf_op jit(solution)/shard_map/ppermute | solution.py:47
  479.5 34.9 %collective-permute-start.21 = (bf16[2,4,128,768]{3,2,0,1:T(8,128)(2,1)S(1)}, bf16[2,4,128,768]{3,2,0,1:T(8,128)(2,1)S(1)}, u32[]{:S(2)}, u32[]{:S(2)}) collective-permute-start(bf16[2,4,128,768]{3,2,0,1:T(8,128)(2,1)S(1)} %fusion.67), channel_id=1, source_target_pairs={{0,4},{1,3},{2,6},{3,1},{4,0},{5,7},{6,2},{7,5},{8,12},{9,11},{10,... | collective-permute-start | bytes 4718600 | tf_op jit(solution)/shard_map/ppermute | solution.py:47
  490.3 93.4 %collective-permute-start.31 = (bf16[4,128,768]{2,1,0:T(8,128)(2,1)}, bf16[4,128,768]{2,1,0:T(8,128)(2,1)}, u32[]{:S(2)}, u32[]{:S(2)}) collective-permute-start(bf16[4,128,768]{2,1,0:T(8,128)(2,1)} %fusion.70), channel_id=1, source_target_pairs={{0,2},{1,5},{2,0},{3,7},{4,6},{5,1},{6,4},{7,3},{8,10},{9,13},{10,... | collective-permute-start | bytes 2359304 | tf_op jit(solution)/shard_map/ppermute | solution.py:47
  516.5 73.6 %collective-permute-start.22 = (bf16[4,128,768]{2,1,0:T(8,128)(2,1)S(1)}, bf16[4,128,768]{2,1,0:T(8,128)(2,1)}, u32[]{:S(2)}, u32[]{:S(2)}) collective-permute-start(bf16[4,128,768]{2,1,0:T(8,128)(2,1)S(1)} %fusion.69), channel_id=1, source_target_pairs={{0,2},{1,5},{2,0},{3,7},{4,6},{5,1},{6,4},{7,3},{8,10},{9,13},{10,... | collective-permute-start | bytes 2359304 | tf_op jit(solution)/shard_map/ppermute | solution.py:47
  590.1 26.5 %collective-permute-start.33 = (bf16[128,768]{1,0:T(8,128)(2,1)S(1)}, bf16[128,768]{1,0:T(8,128)(2,1)S(1)}, u32[]{:S(2)}, u32[]{:S(2)}) collective-permute-start(bf16[128,768]{1,0:T(8,128)(2,1)S(1)} %get-tuple-element.40), channel_id=1, source_target_pairs={{0,16},{1,17},{2,18},{3,19},{4,20},{5,21},{6,22},{7,23},{8,24},{9,... | collective-permute-start | bytes 589832 | tf_op jit(solution)/shard_map/ppermute | solution.py:47
  591.6 26.8 %collective-permute-start.23 = (bf16[128,768]{1,0:T(8,128)(2,1)S(1)}, bf16[128,768]{1,0:T(8,128)(2,1)S(1)}, u32[]{:S(2)}, u32[]{:S(2)}) collective-permute-start(bf16[128,768]{1,0:T(8,128)(2,1)S(1)} %get-tuple-element.41), channel_id=1, source_target_pairs={{0,8},{1,9},{2,10},{3,11},{4,12},{5,13},{6,14},{7,15},{8,0},{9,1},... | collective-permute-start | bytes 589832 | tf_op jit(solution)/shard_map/ppermute | solution.py:47
  594.2 24.7 %collective-permute-start.25 = (bf16[128,768]{1,0:T(8,128)(2,1)S(1)}, bf16[128,768]{1,0:T(8,128)(2,1)S(1)}, u32[]{:S(2)}, u32[]{:S(2)}) collective-permute-start(bf16[128,768]{1,0:T(8,128)(2,1)S(1)} %get-tuple-element.42), channel_id=1, source_target_pairs={{0,24},{1,25},{2,26},{3,27},{4,28},{5,29},{6,30},{7,31},{8,16},{9,... | collective-permute-start | bytes 589832 | tf_op jit(solution)/shard_map/ppermute | solution.py:47
  596.0 28.6 %collective-permute-start.24 = (bf16[128,768]{1,0:T(8,128)(2,1)S(1)}, bf16[128,768]{1,0:T(8,128)(2,1)S(1)}, u32[]{:S(2)}, u32[]{:S(2)}) collective-permute-start(bf16[128,768]{1,0:T(8,128)(2,1)S(1)} %get-tuple-element.43), channel_id=1, source_target_pairs={{0,16},{1,17},{2,18},{3,19},{4,20},{5,21},{6,22},{7,23},{8,24},{9,... | collective-permute-start | bytes 589832 | tf_op jit(solution)/shard_map/ppermute | solution.py:47
  (62 other events, 787.7 us)
Sparse Core Ops, SparseCore 0:
  463.1 116.6 all-reduce.1
where the time goes:
time: 659 us; the launch traced here: 650 us
  local copies, waits for them, and re-layouts  144 us (22%)
  other arithmetic  143 us (22%)
  waiting for transfers between devices  143 us (22%)
  matrix products  119 us (18%)
  blocking collectives  45.8 us (7%)
  starting transfers between devices  40.6 us (6%)
  between operations  15.4 us (2%)
    ppermute x38, waiting for transfers between devices, move(): return lax.ppermute(value, AXES, pairs)  83.7 us
    dot_general x12, matrix products, dot(): return lax.dot_general(a, b, (dims, ((), ())), preferred_element_type=F32)  71.4 us
    psum x1, waiting for transfers between devices, per_device(): smalls = lax.psum(smalls, AXES)  58.8 us
    unnamed x105, local copies, waits for them, and re-layouts  49.5 us
    select_n x12, other arithmetic, flip_if(): return jnp.where(bit == 1, jnp.flip(value, axis), value)  49 us
    all_gather x1, blocking collectives, per_device(): small = lax.all_gather(small, 'batch', axis=1, tiled=True)  45.8 us
    ppermute x38, starting transfers between devices, move(): return lax.ppermute(value, AXES, pairs)  40.5 us
    convert_element_type x2, local copies, waits for them, and re-layouts, per_device(): jnp.stack([g_q, g_k, g_v], axis=2).astype(BF).reshape(-1, 3 * width)  19.5 us
  transfers between devices with their start and end apart: 39, of which 13 were waited for; matrix products, arithmetic and copies ran while one was open for 23% of the time, Pallas kernels for 0%

commit v1 on v0

--- a/solution.py
+++ b/solution.py
@@ -184,7 +184,7 @@
         [gg1, gg2, gb1, gb_packed[:width], gb_packed[2 * width :], gb_out, gb2, gb_down, gb_up]
         + [zero] * 7
     )
-    smalls = lax.psum(smalls, AXES)
+    smalls = jnp.sum(lax.all_gather(smalls, AXES), axis=0)
     smalls = lax.dynamic_slice_in_dim(
         smalls, lax.axis_index("batch") * (width // nb), width // nb, 1
     )

time: 659 us -> 603 us (0.915)
  waiting for transfers between devices: 143 us -> 90 us
    psum x1 -> x0, waiting for transfers between devices: 58.8 us -> none  [per_device(): smalls = lax.psum(smalls, AXES)]
    unnamed x105 -> x103, local copies, waits for them, and re-layouts: 49.5 us -> 49.4 us
  transfers between devices with their start and end apart: 39 -> 39, of which waited for: 13 -> 13; matrix products, arithmetic and copies ran while one was open for 23% -> 25% of each run, Pallas kernels for 0% -> 0%
where the time goes in v1:
time: 603 us; the launch traced here: 595 us
  other arithmetic  146 us (24%)
  local copies, waits for them, and re-layouts  141 us (23%)
  matrix products  119 us (20%)
  waiting for transfers between devices  90 us (15%)
  blocking collectives  45.8 us (8%)
  starting transfers between devices  37.6 us (6%)
  between operations  15.4 us (3%)
    ppermute x38, waiting for transfers between devices, move(): return lax.ppermute(value, AXES, pairs)  90 us
    dot_general x12, matrix products, dot(): return lax.dot_general(a, b, (dims, ((), ())), preferred_element_type=F32)  71.3 us
    unnamed x103, local copies, waits for them, and re-layouts  49.4 us
    select_n x12, other arithmetic, flip_if(): return jnp.where(bit == 1, jnp.flip(value, axis), value)  49 us
    all_gather x1, blocking collectives, per_device(): small = lax.all_gather(small, 'batch', axis=1, tiled=True)  45.8 us
    ppermute x38, starting transfers between devices, move(): return lax.ppermute(value, AXES, pairs)  37.5 us
    convert_element_type x2, local copies, waits for them, and re-layouts, per_device(): jnp.stack([g_q, g_k, g_v], axis=2).astype(BF).reshape(-1, 3 * width)  19.5 us
    sub x1, other arithmetic, per_device(): raised = jnp.exp(scores - top)  19 us
  transfers between devices with their start and end apart: 39, of which 13 were waited for; matrix products, arithmetic and copies ran while one was open for 25% of the time, Pallas kernels for 0%

profile of v1, /device:TPU:0, one launch (start us, length us, event | category | flops | bytes accessed | tf_op | source)
XLA Modules:
  0.0 594.6 jit_solution(3247819331048956905)
XLA Ops:
  20.9 45.8 %all_gather.9 = bf16[9,1024]{1,0:T(8,128)(2,1)S(1)} all-gather(bf16[9,128]{1,0:T(8,128)(2,1)S(1)} %pad_maximum_fusion.9), channel_id=1, replica_groups=mesh['batch'=8,'rep'=4] {'batch'}, dimensions={1}, use_global_device_ids=true | all-gather | bytes 20736 | tf_op jit(solution)/shard_map/all_gather | solution.py:130
  89.4 12.0 %collective-permute-done.14 = bf16[4,32,3072]{2,1,0:T(8,128)(2,1)S(1)} collective-permute-done((bf16[4,32,3072]{2,1,0:T(8,128)(2,1)S(1)}, bf16[4,32,3072]{2,1,0:T(8,128)(2,1)S(1)}, u32[]{:S(2)}, u32[]{:S(2)}) %collective-permute-start.14) | collective-permute-done | bytes 786464 | tf_op jit(solution)/shard_map/ppermute | solution.py:47
  107.8 8.4 %collective-permute-done.15 = bf16[4,32,3072]{2,1,0:T(8,128)(2,1)} collective-permute-done((bf16[4,32,3072]{2,1,0:T(8,128)(2,1)S(1)}, bf16[4,32,3072]{2,1,0:T(8,128)(2,1)}, u32[]{:S(2)}, u32[]{:S(2)}) %collective-permute-start.15) | collective-permute-done | bytes 786464 | tf_op jit(solution)/shard_map/ppermute | solution.py:47
  147.1 7.6 %reverse_select_fusion.7 = bf16[2,2,2,4,32,3072]{5,4,2,0,1,3:T(8,128)(2,1)S(1)} fusion(bf16[2,2,2,4,32,3072]{5,4,2,0,1,3:T(8,128)(2,1)} %reverse_select_fusion.8, pred[]{:T(512)S(6)} %eq.21), kind=kLoop, calls=%fused_computation.17 | loop fusion | flops 3145728 | bytes 12582913 | tf_op jit(solution)/shard_map/jit(_where)/select_n | solution.py:51
  169.1 7.5 %reverse_select_fusion.5 = bf16[2,2,2,2,2,32,3072]{6,5,2,0,1,4,3:T(8,128)(2,1)S(1)} fusion(bf16[2,2,2,2,2,32,3072]{6,5,2,0,1,4,3:T(8,128)(2,1)} %reverse_select_fusion.6, pred[]{:T(512)S(6)} %eq.19), kind=kLoop, calls=%fused_computation.15 | loop fusion | flops 3145728 | bytes 12582913 | tf_op jit(solution)/shard_map/jit(_where)/select_n | solution.py:51
  181.3 8.7 %fusion.5 = bf16[128,8,24,128]{3,1,2,0:T(8,128)(2,1)} fusion(f32[3072]{0:T(1024)S(1)} %pad_maximum_fusion.8, bf16[1024,1024]{1,0:T(8,128)(2,1)S(1)} %bitcast.351, bf16[1024,3072]{1,0:T(8,128)(2,1)S(1)} %bitcast.344), kind=kOutput, calls=%fused_computation.22 | convolution fusion | flops 6448742400 | bytes 14692352 | tf_op jit(solution)/shard_map/dot_general | solution.py:139
  202.4 10.4 %fusion.52 = f32[2,8,512,512]{2,3,1,0:T(8,128)} fusion(bf16[2,512,1,8,128]{4,3,2,1,0:T(8,128)(2,1)} %get-tuple-element.42, bf16[2,512,1,8,128]{4,3,2,1,0:T(8,128)(2,1)} %get-tuple-element.40), kind=kOutput, calls=%fused_computation.106 | convolution fusion | flops 1073741824 | bytes 20971520 | tf_op jit(solution)/shard_map/iqhd,ikhd->ihqk/dot_general | solution.py:147
  212.7 19.0 %fusion.100 = (f32[2,8,512]{2,1,0:T(8,128)S(1)}, f32[2,8,512,512]{2,3,1,0:T(8,128)}) fusion(f32[2,8,512,512]{2,3,1,0:T(8,128)} %fusion.52), kind=kOutput, calls=%fused_computation.208 | output fusion | flops 16777728 | bytes 33587200 | tf_op jit(solution)/shard_map/sub | solution.py:149
  231.8 8.4 %convert_bitcast_fusion.2 = bf16[2,512,8,128]{1,3,2,0:T(8,128)(2,1)} fusion(bf16[2,512,1,8,128]{1,4,3,0,2:T(8,128)(2,1)S(1)} %copy-done.21, f32[2,8,512,512]{2,3,1,0:T(8,128)} %get-tuple-element.83, f32[2,8,512]{2,1,0:T(8,128)S(1)} %get-tuple-element.82), kind=kOutput, calls=%fused_computation.105 | convolution fusion | flops 1083179008 | bytes 21004288 | tf_op jit(solution)/shard_map/ihqk,ikhd->iqhd/dot_general | solution.py:152
  288.0 10.7 %fusion.38 = bf16[2,512,1,8,128]{1,4,3,0,2:T(8,128)(2,1)} fusion(bf16[2,512,8,128]{1,3,2,0:T(8,128)(2,1)} %copy.89, f32[2,8,512,512]{2,3,1,0:T(8,128)} %get-tuple-element.83, f32[2,8,512]{2,1,0:T(8,128)S(1)} %get-tuple-element.82), kind=kOutput, calls=%fused_computation.94 | convolution fusion | flops 1082130432 | bytes 21004288 | tf_op jit(solution)/shard_map/ihqk,iqhd->ikhd/dot_general | solution.py:172
  298.7 10.9 %multiply_reduce_fusion = (f32[2,8,512]{2,1,0:T(8,128)S(1)}, f32[2,8,512,512]{2,3,1,0:T(8,128)}) fusion(f32[2,8,512,512]{2,3,1,0:T(8,128)} %get-tuple-element.83, f32[2,8,512]{2,1,0:T(8,128)S(1)} %get-tuple-element.82, bf16[2,512,8,128]{1,3,2,0:T(8,128)(2,1)S(1)} %copy-done.24, bf16[2,512,1,8,128]{1,4,3,0,2:T(8,128)(2,1)S(1)} %copy-done.22), kind=kOutput, calls=%fused_computation.2 | convolution fusion | flops 1086316544 | bytes 37814272 | tf_op jit(solution)/shard_map/iqhd,ikhd->ihqk/dot_general | solution.py:173
  309.6 11.9 %multiply_convert_fusion = bf16[2,8,512,512]{2,3,1,0:T(8,128)(2,1)S(1)} fusion(f32[2,8,512,512]{2,3,1,0:T(8,128)} %get-tuple-element.88, f32[2,8,512]{2,1,0:T(8,128)S(1)} %get-tuple-element.87, f32[2,8,512,512]{2,3,1,0:T(8,128)} %get-tuple-element.83, f32[2,8,512]{2,1,0:T(8,128)S(1)} %get-tuple-element.82), kind=kLoop, calls=%fused_computation.1 | loop fusion | flops 16777216 | bytes 42008576 | tf_op jit(solution)/shard_map/convert_element_type | solution.py:174
  336.8 16.9 %reshape.233 = f32[4,2,128,2,2,768]{2,1,0,5,4,3:T(2,128)} reshape(f32[1024,3072]{0,1:T(8,128)} %pad_maximum_fusion) | data formatting | bytes 25165824 | tf_op jit(solution)/shard_map/reshape | solution.py:84
  360.3 8.7 %copy.125 = bf16[4,2,128,1,2,768]{5,2,0,1,4,3:T(8,128)(2,1)} copy(bf16[4,2,128,1,2,768]{2,1,0,5,4,3:T(2,128)(2,1)} %constant_dynamic-slice_fusion.1) | data formatting | bytes 6291456
  375.5 9.2 %copy.91 = bf16[2,512,3,8,128]{4,3,2,1,0:T(8,128)(2,1)} copy(bf16[2,512,3,8,128]{1,4,3,0,2:T(8,128)(2,1)} %get-tuple-element.37) | data formatting | bytes 12582912 | tf_op jit(solution)/shard_map/convert_element_type | solution.py:177
  384.6 10.3 %convert_element_type.247 = bf16[1024,3072]{1,0:T(8,128)(2,1)} reshape(bf16[2,512,3,8,128]{4,3,2,1,0:T(8,128)(2,1)} %copy.91) | data formatting | bytes 12582912 | tf_op jit(solution)/shard_map/convert_element_type | solution.py:177
  394.9 12.3 %fusion.93 = (f32[1024]{0:T(1024)S(1)}, f32[1024]{0:T(1024)S(1)}, f32[1024,1024]{1,0:T(8,128)}) fusion(f32[1024]{0:T(1024)S(1)} %bitcast.373, f32[1024]{0:T(1024)S(1)} %bitcast.378, bf16[1,2,512,1024]{3,2,1,0:T(8,128)(2,1)S(1)} %copy-done.2, bf16[1024,3072]{1,0:T(8,128)(2,1)} %convert_element_type.247, bf16[1024,3072]{1,0:T(8,128)(2,1)} %bitcast.345), kind=kOutput, calls=%fused_computation.202 | convolution fusion | flops 6448740352 | bytes 18890752 | tf_op jit(solution)/shard_map/dot_general | solution.py:139
  407.3 8.9 %copy.92 = bf16[3072,1024]{1,0:T(8,128)(2,1)} copy(bf16[3072,1024]{0,1:T(8,128)(2,1)} %bitcast.326) | data formatting | bytes 12582912 | tf_op jit(solution)/shard_map/dot_general | solution.py:139
  425.3 9.5 %fusion.102 = f32[4,2,128,2,2,768]{5,2,4,3,1,0:T(8,128)S(1)} fusion(bf16[4,2,128,1024,1,1]{3,2,5,4,1,0:T(8,128)(2,1)} %bitcast.354, bf16[2,2,768,1024,1,1]{3,2,1,0,5,4:T(8,128)(2,1)} %bitcast.346), kind=kOutput, calls=%fused_computation.210 | convolution fusion | flops 6442450944 | bytes 20971520 | tf_op jit(solution)/shard_map/dot_general | solution.py:139
  443.5 7.6 %constant_dynamic-slice_fusion.2 = f32[4,2,128,1,2,768]{2,1,0,5,4,3:T(2,128)} fusion(f32[4,2,128,2,2,768]{2,1,0,5,4,3:T(2,128)} %reshape.233, s32[]{:T(128)S(6)} %select_n.249), kind=kLoop, calls=%fused_computation.179 | loop fusion | bytes 12582916 | tf_op jit(solution)/shard_map/dynamic-slice.2
  451.1 10.5 %copy.124 = f32[4,2,128,1,2,768]{5,2,0,1,4,3:T(8,128)} copy(f32[4,2,128,1,2,768]{2,1,0,5,4,3:T(2,128)} %constant_dynamic-slice_fusion.2) | data formatting | bytes 12582912
  480.6 8.4 %add_convert_fusion.2 = bf16[1024,1024]{1,0:T(8,128)(2,1)} fusion(f32[1024,1024]{1,0:T(8,128)} %copy-done.10, f32[1024]{0:T(1024)S(1)} %bitcast.396, bf16[1024,3072]{1,0:T(8,128)(2,1)} %bitcast.337, f32[1024,1024]{1,0:T(8,128)} %copy-done.41, f32[1024]{0:T(1024)S(1)} %bitcast.395), kind=kOutput, calls=%fused_computation.75 | convolution fusion | flops 2161115136 | bytes 12591104 | tf_op jit(solution)/shard_map/dot_general | solution.py:139
  491.7 28.2 %collective-permute-done.21 = bf16[2,4,128,768]{3,2,0,1:T(8,128)(2,1)S(1)} collective-permute-done((bf16[2,4,128,768]{3,2,0,1:T(8,128)(2,1)S(1)}, bf16[2,4,128,768]{3,2,0,1:T(8,128)(2,1)S(1)}, u32[]{:S(2)}, u32[]{:S(2)}) %collective-permute-start.21) | collective-permute-done | bytes 1572896 | tf_op jit(solution)/shard_map/ppermute | solution.py:47
  544.2 17.5 %collective-permute-done.33 = bf16[128,768]{1,0:T(8,128)(2,1)S(1)} collective-permute-done((bf16[128,768]{1,0:T(8,128)(2,1)S(1)}, bf16[128,768]{1,0:T(8,128)(2,1)S(1)}, u32[]{:S(2)}, u32[]{:S(2)}) %collective-permute-start.33) | collective-permute-done | bytes 196640 | tf_op jit(solution)/shard_map/ppermute | solution.py:47
  (286 shorter events, 270.0 us)
Async XLA Ops:
  7.2 519.2 %all-gather.3.cloned.1.call-start = ((), (), s32[]{:S(2)}) async-start(), calls=%async_computation | async-start | bytes 2162688 | tf_op jit(solution)/shard_map/all_gather | solution.py:187
  8.3 59.0 %collective-permute-start.2 = (bf16[32,3072]{1,0:T(8,128)(2,1)S(1)}, bf16[32,3072]{1,0:T(8,128)(2,1)S(1)}, u32[]{:S(2)}, u32[]{:S(2)}) collective-permute-start(bf16[32,3072]{1,0:T(8,128)(2,1)S(1)} %fusion.119), channel_id=1, source_target_pairs={{0,24},{1,25},{2,26},{3,27},{4,28},{5,29},{6,30},{7,31},{8,16},{9,... | collective-permute-start | bytes 589832 | tf_op jit(solution)/shard_map/ppermute | solution.py:47
  13.4 54.2 %collective-permute-start.1 = (bf16[32,3072]{1,0:T(8,128)(2,1)S(1)}, bf16[32,3072]{1,0:T(8,128)(2,1)S(1)}, u32[]{:S(2)}, u32[]{:S(2)}) collective-permute-start(bf16[32,3072]{1,0:T(8,128)(2,1)S(1)} %fusion.119), channel_id=1, source_target_pairs={{0,16},{1,17},{2,18},{3,19},{4,20},{5,21},{6,22},{7,23},{8,24},{9,... | collective-permute-start | bytes 589832 | tf_op jit(solution)/shard_map/ppermute | solution.py:47
  13.5 54.2 %collective-permute-start = (bf16[32,3072]{1,0:T(8,128)(2,1)S(1)}, bf16[32,3072]{1,0:T(8,128)(2,1)S(1)}, u32[]{:S(2)}, u32[]{:S(2)}) collective-permute-start(bf16[32,3072]{1,0:T(8,128)(2,1)S(1)} %fusion.119), channel_id=1, source_target_pairs={{0,8},{1,9},{2,10},{3,11},{4,12},{5,13},{6,14},{7,15},{8,0},{9,1},... | collective-permute-start | bytes 589832 | tf_op jit(solution)/shard_map/ppermute | solution.py:47
  16.0 57.5 %collective-permute-start.12 = (bf16[32,3072]{1,0:T(8,128)(2,1)}, bf16[32,3072]{1,0:T(8,128)(2,1)S(1)}, u32[]{:S(2)}, u32[]{:S(2)}) collective-permute-start(bf16[32,3072]{1,0:T(8,128)(2,1)} %fusion.120), channel_id=1, source_target_pairs={{0,24},{1,25},{2,26},{3,27},{4,28},{5,29},{6,30},{7,31},{8,16},{9,... | collective-permute-start | bytes 589832 | tf_op jit(solution)/shard_map/ppermute | solution.py:47
  19.7 53.9 %collective-permute-start.11 = (bf16[32,3072]{1,0:T(8,128)(2,1)}, bf16[32,3072]{1,0:T(8,128)(2,1)S(1)}, u32[]{:S(2)}, u32[]{:S(2)}) collective-permute-start(bf16[32,3072]{1,0:T(8,128)(2,1)} %fusion.120), channel_id=1, source_target_pairs={{0,16},{1,17},{2,18},{3,19},{4,20},{5,21},{6,22},{7,23},{8,24},{9,... | collective-permute-start | bytes 589832 | tf_op jit(solution)/shard_map/ppermute | solution.py:47
  68.6 16.0 %collective-permute-start.4 = (bf16[4,32,3072]{2,1,0:T(8,128)(2,1)}, bf16[4,32,3072]{2,1,0:T(8,128)(2,1)}, u32[]{:S(2)}, u32[]{:S(2)}) collective-permute-start(bf16[4,32,3072]{2,1,0:T(8,128)(2,1)} %get-tuple-element.62), channel_id=1, source_target_pairs={{0,2},{1,5},{2,0},{3,7},{4,6},{5,1},{6,4},{7,3},{8,10},{9,13},{10,... | collective-permute-start | bytes 2359304 | tf_op jit(solution)/shard_map/ppermute | solution.py:47
  70.1 17.6 %collective-permute-start.3 = (bf16[4,32,3072]{2,1,0:T(8,128)(2,1)}, bf16[4,32,3072]{2,1,0:T(8,128)(2,1)}, u32[]{:S(2)}, u32[]{:S(2)}) collective-permute-start(bf16[4,32,3072]{2,1,0:T(8,128)(2,1)} %get-tuple-element.62), channel_id=1, source_target_pairs={{0,4},{1,3},{2,6},{3,1},{4,0},{5,7},{6,2},{7,5},{8,12},{9,11},{10,... | collective-permute-start | bytes 2359304 | tf_op jit(solution)/shard_map/ppermute | solution.py:47
  73.5 48.8 %collective-permute-start.6 = (bf16[4,32,3072]{2,1,0:T(8,128)(2,1)}, bf16[4,32,3072]{2,1,0:T(8,128)(2,1)S(1)}, u32[]{:S(2)}, u32[]{:S(2)}) collective-permute-start(bf16[4,32,3072]{2,1,0:T(8,128)(2,1)} %get-tuple-element.62), channel_id=1, source_target_pairs={{0,1},{1,0},{2,3},{3,2},{4,5},{5,4},{6,7},{7,6},{8,9},{9,8},{10,11... | collective-permute-start | bytes 2359304 | tf_op jit(solution)/shard_map/ppermute | solution.py:47
  74.7 26.7 %collective-permute-start.14 = (bf16[4,32,3072]{2,1,0:T(8,128)(2,1)S(1)}, bf16[4,32,3072]{2,1,0:T(8,128)(2,1)S(1)}, u32[]{:S(2)}, u32[]{:S(2)}) collective-permute-start(bf16[4,32,3072]{2,1,0:T(8,128)(2,1)S(1)} %get-tuple-element.64), channel_id=1, source_target_pairs={{0,2},{1,5},{2,0},{3,7},{4,6},{5,1},{6,4},{7,3},{8,10},{9,13},{10,... | collective-permute-start | bytes 2359304 | tf_op jit(solution)/shard_map/ppermute | solution.py:47
  76.0 25.4 %collective-permute-start.13 = (bf16[4,32,3072]{2,1,0:T(8,128)(2,1)S(1)}, bf16[4,32,3072]{2,1,0:T(8,128)(2,1)S(1)}, u32[]{:S(2)}, u32[]{:S(2)}) collective-permute-start(bf16[4,32,3072]{2,1,0:T(8,128)(2,1)S(1)} %get-tuple-element.64), channel_id=1, source_target_pairs={{0,4},{1,3},{2,6},{3,1},{4,0},{5,7},{6,2},{7,5},{8,12},{9,11},{10,... | collective-permute-start | bytes 2359304 | tf_op jit(solution)/shard_map/ppermute | solution.py:47
  84.6 23.0 %collective-permute-start.5 = (bf16[4,32,3072]{2,1,0:T(8,128)(2,1)}, bf16[4,32,3072]{2,1,0:T(8,128)(2,1)S(1)}, u32[]{:S(2)}, u32[]{:S(2)}) collective-permute-start(bf16[4,32,3072]{2,1,0:T(8,128)(2,1)} %collective-permute-done.4), channel_id=1, source_target_pairs={{0,4},{1,3},{2,6},{3,1},{4,0},{5,7},{6,2},{7,5},{8,12},{9,11},{10,... | collective-permute-start | bytes 2359304 | tf_op jit(solution)/shard_map/ppermute | solution.py:47
  87.7 29.7 %collective-permute-start.8 = (bf16[4,32,3072]{2,1,0:T(8,128)(2,1)}, bf16[4,32,3072]{2,1,0:T(8,128)(2,1)S(1)}, u32[]{:S(2)}, u32[]{:S(2)}) collective-permute-start(bf16[4,32,3072]{2,1,0:T(8,128)(2,1)} %collective-permute-done.4), channel_id=1, source_target_pairs={{0,1},{1,0},{2,3},{3,2},{4,5},{5,4},{6,7},{7,6},{8,9},{9,8},{10,11... | collective-permute-start | bytes 2359304 | tf_op jit(solution)/shard_map/ppermute | solution.py:47
  101.4 16.6 %collective-permute-start.7 = (bf16[4,32,3072]{2,1,0:T(8,128)(2,1)}, bf16[4,32,3072]{2,1,0:T(8,128)(2,1)S(1)}, u32[]{:S(2)}, u32[]{:S(2)}) collective-permute-start(bf16[4,32,3072]{2,1,0:T(8,128)(2,1)} %collective-permute-done.3), channel_id=1, source_target_pairs={{0,1},{1,0},{2,3},{3,2},{4,5},{5,4},{6,7},{7,6},{8,9},{9,8},{10,11... | collective-permute-start | bytes 2359304 | tf_op jit(solution)/shard_map/ppermute | solution.py:47
  101.4 14.8 %collective-permute-start.15 = (bf16[4,32,3072]{2,1,0:T(8,128)(2,1)S(1)}, bf16[4,32,3072]{2,1,0:T(8,128)(2,1)}, u32[]{:S(2)}, u32[]{:S(2)}) collective-permute-start(bf16[4,32,3072]{2,1,0:T(8,128)(2,1)S(1)} %collective-permute-done.14), channel_id=1, source_target_pairs={{0,4},{1,3},{2,6},{3,1},{4,0},{5,7},{6,2},{7,5},{8,12},{9,11},{10,... | collective-permute-start | bytes 2359304 | tf_op jit(solution)/shard_map/ppermute | solution.py:47
  369.0 94.0 %collective-permute-start.29 = (bf16[2,2,4,128,768]{4,3,2,0,1:T(8,128)(2,1)}, bf16[2,2,4,128,768]{4,3,2,0,1:T(8,128)(2,1)}, u32[]{:S(2)}, u32[]{:S(2)}) collective-permute-start(bf16[2,2,4,128,768]{4,3,2,0,1:T(8,128)(2,1)} %bitcast.349), channel_id=1, source_target_pairs={{0,1},{1,0},{2,3},{3,2},{4,5},{5,4},{6,7},{7,6},{8,9},{9,8},{10,11... | collective-permute-start | bytes 9437192 | tf_op jit(solution)/shard_map/ppermute | solution.py:47
  441.4 28.0 %collective-permute-start.20 = (bf16[2,2,4,128,768]{4,3,1,0,2:T(8,128)(2,1)}, bf16[2,2,4,128,768]{4,3,1,0,2:T(8,128)(2,1)}, u32[]{:S(2)}, u32[]{:S(2)}) collective-permute-start(bf16[2,2,4,128,768]{4,3,1,0,2:T(8,128)(2,1)} %fusion.36), channel_id=1, source_target_pairs={{0,1},{1,0},{2,3},{3,2},{4,5},{5,4},{6,7},{7,6},{8,9},{9,8},{10,11... | collective-permute-start | bytes 9437192 | tf_op jit(solution)/shard_map/ppermute | solution.py:47
  468.2 21.0 %collective-permute-start.30 = (bf16[2,4,128,768]{3,2,1,0:T(8,128)(2,1)S(1)}, bf16[2,4,128,768]{3,2,1,0:T(8,128)(2,1)S(1)}, u32[]{:S(2)}, u32[]{:S(2)}) collective-permute-start(bf16[2,4,128,768]{3,2,1,0:T(8,128)(2,1)S(1)} %fusion.68), channel_id=1, source_target_pairs={{0,4},{1,3},{2,6},{3,1},{4,0},{5,7},{6,2},{7,5},{8,12},{9,11},{10,... | collective-permute-start | bytes 4718600 | tf_op jit(solution)/shard_map/ppermute | solution.py:47
  479.6 40.4 %collective-permute-start.21 = (bf16[2,4,128,768]{3,2,0,1:T(8,128)(2,1)S(1)}, bf16[2,4,128,768]{3,2,0,1:T(8,128)(2,1)S(1)}, u32[]{:S(2)}, u32[]{:S(2)}) collective-permute-start(bf16[2,4,128,768]{3,2,0,1:T(8,128)(2,1)S(1)} %fusion.67), channel_id=1, source_target_pairs={{0,4},{1,3},{2,6},{3,1},{4,0},{5,7},{6,2},{7,5},{8,12},{9,11},{10,... | collective-permute-start | bytes 4718600 | tf_op jit(solution)/shard_map/ppermute | solution.py:47
  490.6 39.3 %collective-permute-start.31 = (bf16[4,128,768]{2,1,0:T(8,128)(2,1)}, bf16[4,128,768]{2,1,0:T(8,128)(2,1)}, u32[]{:S(2)}, u32[]{:S(2)}) collective-permute-start(bf16[4,128,768]{2,1,0:T(8,128)(2,1)} %fusion.70), channel_id=1, source_target_pairs={{0,2},{1,5},{2,0},{3,7},{4,6},{5,1},{6,4},{7,3},{8,10},{9,13},{10,... | collective-permute-start | bytes 2359304 | tf_op jit(solution)/shard_map/ppermute | solution.py:47
  533.6 28.0 %collective-permute-start.33 = (bf16[128,768]{1,0:T(8,128)(2,1)S(1)}, bf16[128,768]{1,0:T(8,128)(2,1)S(1)}, u32[]{:S(2)}, u32[]{:S(2)}) collective-permute-start(bf16[128,768]{1,0:T(8,128)(2,1)S(1)} %get-tuple-element.49), channel_id=1, source_target_pairs={{0,16},{1,17},{2,18},{3,19},{4,20},{5,21},{6,22},{7,23},{8,24},{9,... | collective-permute-start | bytes 589832 | tf_op jit(solution)/shard_map/ppermute | solution.py:47
  537.2 25.9 %collective-permute-start.23 = (bf16[128,768]{1,0:T(8,128)(2,1)S(1)}, bf16[128,768]{1,0:T(8,128)(2,1)S(1)}, u32[]{:S(2)}, u32[]{:S(2)}) collective-permute-start(bf16[128,768]{1,0:T(8,128)(2,1)S(1)} %get-tuple-element.50), channel_id=1, source_target_pairs={{0,8},{1,9},{2,10},{3,11},{4,12},{5,13},{6,14},{7,15},{8,0},{9,1},... | collective-permute-start | bytes 589832 | tf_op jit(solution)/shard_map/ppermute | solution.py:47
  539.9 24.1 %collective-permute-start.25 = (bf16[128,768]{1,0:T(8,128)(2,1)S(1)}, bf16[128,768]{1,0:T(8,128)(2,1)S(1)}, u32[]{:S(2)}, u32[]{:S(2)}) collective-permute-start(bf16[128,768]{1,0:T(8,128)(2,1)S(1)} %get-tuple-element.51), channel_id=1, source_target_pairs={{0,24},{1,25},{2,26},{3,27},{4,28},{5,29},{6,30},{7,31},{8,16},{9,... | collective-permute-start | bytes 589832 | tf_op jit(solution)/shard_map/ppermute | solution.py:47
  544.2 23.3 %collective-permute-start.24 = (bf16[128,768]{1,0:T(8,128)(2,1)S(1)}, bf16[128,768]{1,0:T(8,128)(2,1)S(1)}, u32[]{:S(2)}, u32[]{:S(2)}) collective-permute-start(bf16[128,768]{1,0:T(8,128)(2,1)S(1)} %get-tuple-element.52), channel_id=1, source_target_pairs={{0,16},{1,17},{2,18},{3,19},{4,20},{5,21},{6,22},{7,23},{8,24},{9,... | collective-permute-start | bytes 589832 | tf_op jit(solution)/shard_map/ppermute | solution.py:47
  (61 other events, 810.7 us)
Sparse Core Ops, SparseCore 0:
  463.1 58.3 all-gather.2
